TPU v7x, 256 devices: a whole 4x4x8 slice. The times are simulated.
256 devices in a mesh: row: 8 (over x, core), col: 32 (over z, y).
Axes of the slice: x: 4, y: 4, z: 8, core: 2. Of those that a mesh axis runs over, the one named last changes fastest.
Arguments:
- panel: bfloat16 [65536, 512], P('row', 'col'), may hold values from -0.0234375 to 0.0234375
- pheno: bfloat16 [65536, 8192], P('row', 'col'), may hold values from -48 to 48
- kin_values: float32 [512], replicated, may hold values from 0.1 to 10
- trait_values: float32 [128], replicated, may hold values from 0.1 to 10
- trait_basis: float32 [128, 128], replicated, may hold values from -0.5 to 0.5
Outputs:
- coeffs: float32 [512, 8192], P('row', 'col')
- genetic: bfloat16 [65536, 8192], P('row', 'col')
All inputs are finite; a program needn't handle non-finite values.
Results may differ from a plain program's by a relative error of at most 0.0049.
Values may be sent and summed in bfloat16 or wider, within the bound.
No kernel may reach another device: no remote copies, remote signals or barrier semaphores. Data moves between devices by JAX's collectives and lax.ppermute only.
A program may use at most 64 MiB of HBM per device.

v0:
```python
import jax
import jax.numpy as jnp
from jax import lax
from jax.sharding import PartitionSpec as P

TRAITS = 128
SETS_DEV = 2


def cut_along(shard, dim, count):
    before, after = (shard.shape[:dim], shard.shape[dim + 1 :])
    return jnp.moveaxis(shard.reshape(*before, count, -1, *after), dim, 0)


def sum_at_owner(shard, axis, dim):
    count = lax.axis_size(axis)
    pieces = lax.all_to_all(cut_along(shard, dim, count), axis, 0, 0, tiled=True)
    return jnp.sum(pieces, axis=0)


def laid_out(pieces, dim):
    dims = list(pieces.shape[1:])
    dims[dim] *= pieces.shape[0]
    return jnp.moveaxis(pieces, 0, dim).reshape(dims)


def copy_for_each(shard, axis):
    count = lax.axis_size(axis)
    return lax.all_to_all(
        jnp.broadcast_to(shard[None], (count, *shard.shape)), axis, 0, 0, tiled=True
    )


def gather_directly(shard, axis, dim):
    return laid_out(copy_for_each(shard, axis), dim)


def local(panel, pheno, kin_values, trait_values, trait_basis):
    col_count = lax.axis_size("col")
    columns = pheno.shape[1]
    traits_here = TRAITS // col_count
    set_count = SETS_DEV * col_count
    whole_panel = lax.all_gather(panel, "col", axis=1, tiled=True)
    partial_value = lax.dot_general(
        whole_panel, pheno, (((0,), (0,)), ((), ())), preferred_element_type=jnp.float32
    )
    summed = sum_at_owner(partial_value, "row", 0)
    first_row = lax.axis_index("row") * summed.shape[0]
    share_rows = summed.shape[0]
    by_trait = summed.reshape(share_rows, traits_here, set_count).transpose(0, 2, 1)
    by_trait = by_trait.reshape(share_rows, set_count * traits_here)
    grouped = lax.all_to_all(by_trait, "col", split_axis=1, concat_axis=1, tiled=True)
    grouped = grouped.reshape(share_rows, col_count, SETS_DEV, traits_here).transpose(0, 2, 1, 3)
    grouped = grouped.reshape(share_rows, SETS_DEV, TRAITS)
    rotated = jnp.einsum("rst,tj->rsj", grouped, trait_basis, precision=lax.Precision.HIGHEST)
    kin_rows = lax.dynamic_slice_in_dim(kin_values, first_row, share_rows, 0)
    product = kin_rows[:, None] * trait_values[None, :]
    scaled = rotated * (product / (product + 1.0))[:, None, :]
    unrotated = jnp.einsum("rsj,tj->rst", scaled, trait_basis, precision=lax.Precision.HIGHEST)
    outgoing = unrotated.reshape(share_rows, SETS_DEV, col_count, traits_here).transpose(0, 2, 1, 3)
    outgoing = outgoing.reshape(share_rows, col_count * SETS_DEV * traits_here)
    returned = lax.all_to_all(outgoing, "col", split_axis=1, concat_axis=1, tiled=True)
    coeffs = returned.reshape(share_rows, set_count, traits_here).transpose(0, 2, 1)
    coeffs = coeffs.reshape(share_rows, columns)
    coeffs_low = gather_directly(coeffs.astype(jnp.bfloat16), "row", 0)
    genetic = jnp.dot(whole_panel, coeffs_low, preferred_element_type=jnp.float32)
    return (coeffs, genetic.astype(jnp.bfloat16))


def solution(mesh):
    return jax.shard_map(
        local,
        mesh=mesh,
        in_specs=(P("row", "col"), P("row", "col"), P(), P(), P()),
        out_specs=(P("row", "col"), P("row", "col")),
        check_vma=False,
    )
```

profile of v0, /device:TPU:1, one launch (start us, length us, event | category | flops | bytes accessed | tf_op | source)
XLA Modules:
  0.0 199.2 jit_solution(6438156583780600088)
XLA Ops:
  7.2 0.7 all-gather.2.cloned.1.call-update
  7.9 104.7 %all-gather.2.cloned.1.call-done = bf16[8192,512]{0,1:T(8,128)(2,1)} async-done(((bf16[8192,16]{0,1:T(8,128)(2,1)}), bf16[8192,512]{0,1:T(8,128)(2,1)}) %all-gather.2.cloned.1.call-update) | async-done | bytes 8388624 | tf_op jit(solution)/shard_map/all_gather | solution.py:43
  112.6 7.7 %fusion.4 = f32[512,256]{1,0:T(8,128)} fusion(bf16[8192,512]{0,1:T(8,128)(2,1)} %all-gather.2.cloned.1.call-done, bf16[8192,256]{1,0:T(8,128)(2,1)} %param.6), kind=kOutput, calls=%fused_computation.9 | convolution fusion | flops 2147483648 | bytes 13107200 | tf_op jit(solution)/shard_map/dot_general | solution.py:44
  120.3 5.3 %all-to-all-start = ((f32[8,64,256]{2,1,0:T(8,128)}), f32[8,64,256]{2,1,0:T(8,128)S(1)}, u32[]{:S(2)}, u32[]{:S(2)}) async-start(f32[8,64,256]{2,1,0:T(8,128)} %bitcast), calls=%async_computation | async-start | bytes 1048576 | tf_op jit(solution)/shard_map/all_to_all | solution.py:17
  125.6 0.8 dynamic_slice.3
  126.4 8.7 %all-to-all-done = f32[8,64,256]{2,1,0:T(8,128)S(1)} async-done(((f32[8,64,256]{2,1,0:T(8,128)}), f32[8,64,256]{2,1,0:T(8,128)S(1)}, u32[]{:S(2)}, u32[]{:S(2)}) %all-to-all-start) | async-done | bytes 524320 | tf_op jit(solution)/shard_map/all_to_all | solution.py:17
  135.1 0.1 reshape.69
  135.2 0.1 copy.23
  135.4 0.8 reshape.77
  136.1 5.3 %all-to-all-start.1 = ((f32[32,1,512]{2,1,0:T(1,128)}), f32[32,1,512]{2,1,0:T(1,128)S(1)}, u32[]{:S(2)}, u32[]{:S(2)}) async-start(f32[32,1,512]{2,1,0:T(1,128)} %reshape.77), calls=%async_computation.1 | async-start | bytes 131072 | tf_op jit(solution)/shard_map/all_to_all | solution.py:52
  141.6 8.7 %all-to-all-done.1 = f32[32,1,512]{2,1,0:T(1,128)S(1)} async-done(((f32[32,1,512]{2,1,0:T(1,128)}), f32[32,1,512]{2,1,0:T(1,128)S(1)}, u32[]{:S(2)}, u32[]{:S(2)}) %all-to-all-start.1) | async-done | bytes 65568 | tf_op jit(solution)/shard_map/all_to_all | solution.py:52
  150.3 0.5 broadcast.18
  150.8 0.8 reduce
  151.8 0.1 copy.25
  151.9 0.4 convolution_multiply_fusion
  152.3 0.3 fusion.1
  152.7 0.1 reshape.79
  152.8 12.0 %all_to_all.28 = f32[32,1,512]{2,1,0:T(1,128)S(1)} all-to-all(f32[32,1,512]{2,1,0:T(1,128)S(1)} %reshape.79), channel_id=1, replica_groups=mesh['row'=8,'col'=32] {'col'}, dimensions={0} | all-to-all | bytes 131072 | tf_op jit(solution)/shard_map/all_to_all | solution.py:62
  164.8 0.8 reduce.1
  165.7 0.1 copy.30
  165.8 0.1 reshape.74
  166.0 12.3 %all_to_all.29 = bf16[8,64,256]{2,1,0:T(8,128)(2,1)S(1)} all-to-all(bf16[8,64,256]{2,1,0:T(8,128)(2,1)S(1)} %broadcast_in_dim.2), channel_id=1, replica_groups=mesh['row'=8,'col'=32] {'row'}, dimensions={0} | all-to-all | bytes 524288 | tf_op jit(solution)/shard_map/all_to_all | solution.py:29
  178.3 7.7 %fusion = bf16[8192,256]{0,1:T(8,128)(2,1)} fusion(bf16[512,256]{1,0:T(8,128)(2,1)S(1)} %bitcast.37, bf16[8192,512]{0,1:T(8,128)(2,1)} %all-gather.2.cloned.1.call-done), kind=kOutput, calls=%fused_computation.1 | convolution fusion | flops 2149580800 | bytes 12845056 | tf_op jit(solution)/shard_map/dot_general | solution.py:66
  186.0 6.4 %copy.31 = bf16[8192,256]{1,0:T(8,128)(2,1)} copy(bf16[8192,256]{0,1:T(8,128)(2,1)} %fusion) | data formatting | bytes 8388608
  (17 shorter events, 0.5 us)
Async XLA Ops:
  7.2 144.7 %copy-start = (f32[128,128]{1,0:T(8,128)S(1)}, f32[128,128]{1,0:T(8,128)}, u32[]{:S(2)}) copy-start(f32[128,128]{1,0:T(8,128)} %param.9) | copy-start | bytes 196612
  7.2 105.4 %all-gather.2.cloned.1.call-start = ((), (), s32[]{:S(2)}) async-start(), calls=%async_computation.4 | async-start | bytes 8650752 | tf_op jit(solution)/shard_map/all_gather | solution.py:43
  7.9 133.6 %copy-start.2 = (f32[128]{0:T(128)S(1)}, f32[128]{0:T(128)}, u32[]{:S(2)}) copy-start(f32[128]{0:T(128)} %param.8) | copy-start | bytes 1540
  120.3 14.8 %all-to-all-start = ((f32[8,64,256]{2,1,0:T(8,128)}), f32[8,64,256]{2,1,0:T(8,128)S(1)}, u32[]{:S(2)}, u32[]{:S(2)}) async-start(f32[8,64,256]{2,1,0:T(8,128)} %bitcast), calls=%async_computation | async-start | bytes 1048576 | tf_op jit(solution)/shard_map/all_to_all | solution.py:17
  136.1 14.2 %all-to-all-start.1 = ((f32[32,1,512]{2,1,0:T(1,128)}), f32[32,1,512]{2,1,0:T(1,128)S(1)}, u32[]{:S(2)}, u32[]{:S(2)}) async-start(f32[32,1,512]{2,1,0:T(1,128)} %reshape.77), calls=%async_computation.1 | async-start | bytes 131072 | tf_op jit(solution)/shard_map/all_to_all | solution.py:52
  166.0 26.4 %copy-start.1 = (f32[64,256]{1,0:T(8,128)}, f32[64,256]{1,0:T(8,128)S(1)}, u32[]{:S(2)}) copy-start(f32[64,256]{1,0:T(8,128)S(1)} %reshape.74) | copy-start | bytes 196612
Sparse Core Ops, SparseCore 0:
  10.6 101.9 all-gather.1
where the time goes:
time: 200 us; the launch traced here: 199 us
  waiting for transfers between devices  123 us (62%)
  blocking collectives  24.2 us (12%)
  matrix products  16.1 us (8%)
  between operations  14.2 us (7%)
  starting transfers between devices  10.7 us (5%)
  local copies, waits for them, and re-layouts  9.41 us (5%)
    all_gather x1, waiting for transfers between devices, local(): whole_panel = lax.all_gather(panel, 'col', axis=1, tiled=True)  105 us
    all_to_all x1, blocking collectives, copy_for_each(): lax.all_to_all(jnp.broadcast_to(shard[None], (count, *shard.shape)), axis...  12.3 us
    all_to_all x1, blocking collectives, local(): lax.all_to_all(outgoing, 'col', split_axis=1, concat_axis=1, tiled=True)  12 us
    all_to_all x1, waiting for transfers between devices, local(): lax.all_to_all(by_trait, 'col', split_axis=1, concat_axis=1, tiled=True)  8.74 us
    all_to_all x1, waiting for transfers between devices, sum_at_owner(): lax.all_to_all(cut_along(shard, dim, count), axis, 0, 0, tiled=True)  8.73 us
    dot_general x1, matrix products, local(): jnp.dot(whole_panel, coeffs_low, preferred_element_type=jnp.float32)  7.71 us
    dot_general x1, matrix products, local(): lax.dot_general(whole_panel, pheno, (((0,), (0,)), ((), ())), preferred_e...  7.7 us
    unnamed x12, local copies, waits for them, and re-layouts  7.44 us
  transfers between devices with their start and end apart: 3, of which 3 were waited for; matrix products, arithmetic and copies ran while one was open for 0% of the time, Pallas kernels for 0%

commit v1 on v0

--- a/solution.py
+++ b/solution.py
@@ -40,7 +40,10 @@
     columns = pheno.shape[1]
     traits_here = TRAITS // col_count
     set_count = SETS_DEV * col_count
-    whole_panel = lax.all_gather(panel, "col", axis=1, tiled=True)
+    count_2 = lax.axis_size("col")
+    blocks = jnp.stack([panel for _ in range(count_2)])
+    blocks = lax.all_to_all(blocks, "col", split_axis=0, concat_axis=0)
+    whole_panel = jnp.concatenate(blocks, axis=1)
     partial_value = lax.dot_general(
         whole_panel, pheno, (((0,), (0,)), ((), ())), preferred_element_type=jnp.float32
     )

time: 200 us -> 279 us (1.40)
  blocking collectives: 24.2 us -> 220 us
  waiting for transfers between devices: 123 us -> 17.5 us
  between operations: 14.2 us -> 0.8 us
  local copies, waits for them, and re-layouts: 9.41 us -> 14.6 us
  matrix products: 16.1 us -> 11.6 us
    all_to_all x0 -> x1, blocking collectives: none -> 196 us  [local(): blocks = lax.all_to_all(blocks, 'col', split_axis=0, concat_axis=0)]
    all_gather x1 -> x0, waiting for transfers between devices: 105 us -> none  [local(): whole_panel = lax.all_gather(panel, 'col', axis=1, tiled=True)]
    dot_general x1, matrix products: 7.7 us -> 3.12 us  [local(): lax.dot_general(whole_panel, pheno, (((0,), (0,)), ((), ())), preferred_e...]
    unnamed x12 -> x16, local copies, waits for them, and re-layouts: 7.44 us -> 10.7 us
  transfers between devices with their start and end apart: 3 -> 2, of which waited for: 3 -> 2; matrix products, arithmetic and copies ran while one was open for 0% -> 0% of each run, Pallas kernels for 0% -> 0%
where the time goes in v1:
time: 279 us; the launch traced here: 278 us
  blocking collectives  220 us (79%)
  waiting for transfers between devices  17.5 us (6%)
  local copies, waits for them, and re-layouts  14.6 us (5%)
  starting transfers between devices  12.4 us (4%)
  matrix products  11.6 us (4%)
    all_to_all x1, blocking collectives, local(): blocks = lax.all_to_all(blocks, 'col', split_axis=0, concat_axis=0)  196 us
    all_to_all x1, blocking collectives, copy_for_each(): lax.all_to_all(jnp.broadcast_to(shard[None], (count, *shard.shape)), axis...  12.3 us
    all_to_all x1, blocking collectives, local(): lax.all_to_all(outgoing, 'col', split_axis=1, concat_axis=1, tiled=True)  12 us
    unnamed x16, local copies, waits for them, and re-layouts  10.7 us
    all_to_all x1, waiting for transfers between devices, local(): lax.all_to_all(by_trait, 'col', split_axis=1, concat_axis=1, tiled=True)  8.74 us
    all_to_all x1, waiting for transfers between devices, sum_at_owner(): lax.all_to_all(cut_along(shard, dim, count), axis, 0, 0, tiled=True)  8.73 us
    dot_general x1, matrix products, local(): jnp.dot(whole_panel, coeffs_low, preferred_element_type=jnp.float32)  7.73 us
    all_to_all x1, starting transfers between devices, sum_at_owner(): lax.all_to_all(cut_along(shard, dim, count), axis, 0, 0, tiled=True)  7.13 us
  transfers between devices with their start and end apart: 2, of which 2 were waited for; matrix products, arithmetic and copies ran while one was open for 0% of the time, Pallas kernels for 0%

profile of v1, /device:TPU:1, one launch (start us, length us, event | category | flops | bytes accessed | tf_op | source)
XLA Modules:
  0.0 278.4 jit_solution(1168422730093412155)
XLA Ops:
  0.6 2.0 stack.2
  2.6 195.6 %all_to_all.33 = bf16[32,8192,16]{1,2,0:T(8,128)(2,1)S(1)} all-to-all(bf16[32,8192,16]{1,2,0:T(8,128)(2,1)S(1)} %stack.2), channel_id=1, replica_groups=mesh['row'=8,'col'=32] {'col'}, dimensions={0} | all-to-all | bytes 16777216 | tf_op jit(solution)/shard_map/all_to_all | solution.py:45
  198.3 3.2 %copy-done.1 = bf16[32,8192,16]{1,2,0:T(8,128)(2,1)} copy-done((bf16[32,8192,16]{1,2,0:T(8,128)(2,1)}, bf16[32,8192,16]{1,2,0:T(8,128)(2,1)S(1)}, u32[]{:S(2)}) %copy-start.1) | copy-done | bytes 8388632
  201.5 3.1 %fusion.1 = f32[8,64,256]{2,1,0:T(8,128)} fusion(bf16[8,64,8192]{2,1,0:T(8,128)(2,1)S(1)} %bitcast.45, bf16[8192,256]{1,0:T(8,128)(2,1)S(1)} %copy-done.4), kind=kOutput, calls=%fused_computation.2 | convolution fusion | flops 2147483648 | bytes 13107200 | tf_op jit(solution)/shard_map/dot_general | solution.py:47
  204.6 7.1 %all-to-all-start.1 = ((f32[8,64,256]{2,1,0:T(8,128)}), f32[8,64,256]{2,1,0:T(8,128)S(1)}, u32[]{:S(2)}, u32[]{:S(2)}) async-start(f32[8,64,256]{2,1,0:T(8,128)} %fusion.1), calls=%async_computation.1 | async-start | bytes 1048576 | tf_op jit(solution)/shard_map/all_to_all | solution.py:17
  211.7 0.8 dynamic_slice.3
  212.5 8.7 %all-to-all-done.1 = f32[8,64,256]{2,1,0:T(8,128)S(1)} async-done(((f32[8,64,256]{2,1,0:T(8,128)}), f32[8,64,256]{2,1,0:T(8,128)S(1)}, u32[]{:S(2)}, u32[]{:S(2)}) %all-to-all-start.1) | async-done | bytes 524320 | tf_op jit(solution)/shard_map/all_to_all | solution.py:17
  221.2 0.1 reshape.77
  221.4 0.1 copy.23
  221.5 0.8 reshape.86
  222.3 5.3 %all-to-all-start.2 = ((f32[32,1,512]{2,1,0:T(1,128)}), f32[32,1,512]{2,1,0:T(1,128)S(1)}, u32[]{:S(2)}, u32[]{:S(2)}) async-start(f32[32,1,512]{2,1,0:T(1,128)} %reshape.86), calls=%async_computation.2 | async-start | bytes 131072 | tf_op jit(solution)/shard_map/all_to_all | solution.py:55
  227.6 8.7 %all-to-all-done.2 = f32[32,1,512]{2,1,0:T(1,128)S(1)} async-done(((f32[32,1,512]{2,1,0:T(1,128)}), f32[32,1,512]{2,1,0:T(1,128)S(1)}, u32[]{:S(2)}, u32[]{:S(2)}) %all-to-all-start.2) | async-done | bytes 65568 | tf_op jit(solution)/shard_map/all_to_all | solution.py:55
  236.4 0.5 broadcast.20
  236.9 0.8 reduce
  237.9 0.4 convolution_multiply_fusion
  238.3 0.3 fusion.3
  238.7 0.1 reshape.88
  238.9 12.0 %all_to_all.34 = f32[32,1,512]{2,1,0:T(1,128)S(1)} all-to-all(f32[32,1,512]{2,1,0:T(1,128)S(1)} %reshape.88), channel_id=1, replica_groups=mesh['row'=8,'col'=32] {'col'}, dimensions={0} | all-to-all | bytes 131072 | tf_op jit(solution)/shard_map/all_to_all | solution.py:65
  250.9 0.8 reduce.1
  251.7 0.1 copy.30
  251.9 0.1 reshape.82
  252.0 12.3 %all_to_all.35 = bf16[8,64,256]{2,1,0:T(8,128)(2,1)S(1)} all-to-all(bf16[8,64,256]{2,1,0:T(8,128)(2,1)S(1)} %broadcast_in_dim.2), channel_id=1, replica_groups=mesh['row'=8,'col'=32] {'row'}, dimensions={0} | all-to-all | bytes 524288 | tf_op jit(solution)/shard_map/all_to_all | solution.py:29
  264.3 7.7 %fusion = bf16[8192,256]{0,1:T(8,128)(2,1)} fusion(bf16[512,256]{1,0:T(8,128)(2,1)S(1)} %bitcast.47, bf16[8192,512]{0,1:T(8,128)(2,1)} %bitcast.46), kind=kOutput, calls=%fused_computation.1 | convolution fusion | flops 2149580800 | bytes 12845056 | tf_op jit(solution)/shard_map/dot_general | solution.py:69
  272.0 6.4 %copy.31 = bf16[8192,256]{1,0:T(8,128)(2,1)} copy(bf16[8192,256]{0,1:T(8,128)(2,1)} %fusion) | data formatting | bytes 8388608
  (20 shorter events, 0.6 us)
Async XLA Ops:
  0.6 237.3 %copy-start = (f32[128,128]{1,0:T(8,128)S(1)}, f32[128,128]{1,0:T(8,128)}, u32[]{:S(2)}) copy-start(f32[128,128]{1,0:T(8,128)} %param.9) | copy-start | bytes 196612
  2.6 198.8 %copy-start.4 = (bf16[8192,256]{1,0:T(8,128)(2,1)S(1)}, bf16[8192,256]{1,0:T(8,128)(2,1)}, u32[]{:S(2)}) copy-start(bf16[8192,256]{1,0:T(8,128)(2,1)} %param.6) | copy-start | bytes 12582916
  198.2 3.2 %copy-start.1 = (bf16[32,8192,16]{1,2,0:T(8,128)(2,1)}, bf16[32,8192,16]{1,2,0:T(8,128)(2,1)S(1)}, u32[]{:S(2)}) copy-start(bf16[32,8192,16]{1,2,0:T(8,128)(2,1)S(1)} %all_to_all.33) | copy-start | bytes 25165828
  201.5 26.1 %copy-start.3 = (f32[128]{0:T(128)S(1)}, f32[128]{0:T(128)}, u32[]{:S(2)}) copy-start(f32[128]{0:T(128)} %param.8) | copy-start | bytes 1540
  204.6 16.6 %all-to-all-start.1 = ((f32[8,64,256]{2,1,0:T(8,128)}), f32[8,64,256]{2,1,0:T(8,128)S(1)}, u32[]{:S(2)}, u32[]{:S(2)}) async-start(f32[8,64,256]{2,1,0:T(8,128)} %fusion.1), calls=%async_computation.1 | async-start | bytes 1048576 | tf_op jit(solution)/shard_map/all_to_all | solution.py:17
  222.3 14.1 %all-to-all-start.2 = ((f32[32,1,512]{2,1,0:T(1,128)}), f32[32,1,512]{2,1,0:T(1,128)S(1)}, u32[]{:S(2)}, u32[]{:S(2)}) async-start(f32[32,1,512]{2,1,0:T(1,128)} %reshape.86), calls=%async_computation.2 | async-start | bytes 131072 | tf_op jit(solution)/shard_map/all_to_all | solution.py:55
  252.0 26.4 %copy-start.2 = (f32[64,256]{1,0:T(8,128)}, f32[64,256]{1,0:T(8,128)S(1)}, u32[]{:S(2)}) copy-start(f32[64,256]{1,0:T(8,128)S(1)} %reshape.82) | copy-start | bytes 196612
